TPU v7x, 32 devices: a whole 2x2x4 slice. The times are simulated.
32 devices in a mesh: prow: 4 (over y, core), pcol: 8 (over z, x).
Axes of the slice: x: 2, y: 2, z: 4, core: 2. Of those that a mesh axis runs over, the one named last changes fastest.
Arguments:
- ainv_trail: float32 [2048, 2048], P('prow', 'pcol')
- panel_parent: float32 [2048, 256], P('prow', 'pcol'), may hold values from -0.125 to 0.125
- panel_child: float32 [2048, 256], P('prow', 'pcol'), may hold values from -0.125 to 0.125
- link_block: float32 [256, 256], replicated, may hold values from -0.375 to 0.375
- dinv_parent: float32 [256, 256], replicated
- dinv_child: float32 [256, 256], replicated
- pattern_parent: int32 [8], replicated, may hold values from 0 to 1, as said below
- pattern_child: int32 [8], replicated, may hold values from 0 to 1, as said below
Outputs:
- row_parent: float32 [256, 2048], P('prow', 'pcol')
- diag_parent: float32 [256, 256], P('prow')
- cross_child: float32 [256, 256], P('prow')
- row_child: float32 [256, 2048], P('prow', 'pcol')
- diag_child: float32 [256, 256], P('prow')
Inputs may be any that keep to these rules, and one draw needn't show every extreme that they name: `pattern_parent`: each entry is 0 or 1; the first entry is 1 and at least one entry is 0. `pattern_child`: each entry is 0 or 1, and is 1 only where pattern_parent is 1; the first entry is 1.
All inputs are finite; a program needn't handle non-finite values.
Results may differ from a plain program's by a relative error of at most 0.00009.
Values sent between devices are 32-bit elements; how exact they have to be, the bound alone decides.
A program may use at most 64 MiB of HBM per device.

v0:
```python
import jax
import jax.numpy as jnp
from jax import lax
from jax.sharding import PartitionSpec as P

highest = lax.Precision.HIGHEST


def lead_product(left, right):
    return lax.dot_general(
        left, right, (((0,), (0,)), ((), ())), precision=highest, preferred_element_type=jnp.float32
    )


def plain_product(left, right):
    return jnp.dot(left, right, precision=highest, preferred_element_type=jnp.float32)


def block_mask(pattern, first, count, width):
    picked = lax.dynamic_slice(pattern, (first,), (count,)).astype(jnp.float32)
    return jnp.repeat(picked, width)


def row_total(partial_value, columns, row_index, share):
    total = lax.psum(partial_value, "prow")
    whole = -total * columns[None, :]
    return (lax.dynamic_slice_in_dim(whole, row_index * share, share, 0), whole)


def total_terms(stacked):
    return lax.psum(stacked, ("prow", "pcol"))


def column_terms(row_part, blocks):
    result = plain_product(row_part, blocks[0])
    return result


def on_device(
    ainv_trail,
    panel_parent,
    panel_child,
    link_block,
    dinv_parent,
    dinv_child,
    pattern_parent,
    pattern_child,
):
    width = link_block.shape[0]
    row_count = lax.axis_size("prow")
    row_index = lax.axis_index("prow")
    col_index = lax.axis_index("pcol")
    row_blocks = ainv_trail.shape[0] // width
    col_blocks = ainv_trail.shape[1] // width
    share = width // row_count
    first_row = row_index * row_blocks
    first_col = col_index * col_blocks
    parent_whole, child_whole = (
        lax.all_gather(panel_parent, "pcol", axis=1, tiled=True),
        lax.all_gather(panel_child, "pcol", axis=1, tiled=True),
    )
    parent_rows = parent_whole * block_mask(pattern_parent, first_row, row_blocks, width)[:, None]
    child_rows = child_whole * block_mask(pattern_child, first_row, row_blocks, width)[:, None]
    parent_cols = block_mask(pattern_parent, first_col, col_blocks, width)
    child_cols = block_mask(pattern_child, first_col, col_blocks, width)
    parent_partial = lead_product(parent_rows, ainv_trail)
    child_partial = lead_product(child_rows, ainv_trail)
    link_share = lax.dynamic_slice_in_dim(link_block, row_index * share, share, 0)
    block = first_col + 0
    root = block // row_blocks
    local = jnp.clip(block - first_row, 0, row_blocks - 1)
    parent_piece = lax.dynamic_slice_in_dim(parent_rows, local * width, width, 0)
    child_piece = lax.dynamic_slice_in_dim(child_rows, local * width, width, 0)
    owner = (root == row_index).astype(jnp.float32)
    parent_piece = parent_piece * owner
    child_piece = child_piece * owner
    parent_blocks = [parent_piece]
    child_blocks = [child_piece]
    parent_share, parent_part = row_total(parent_partial, parent_cols, row_index, share)
    first_terms = total_terms(
        jnp.stack(
            [column_terms(parent_part, parent_blocks), column_terms(parent_part, child_blocks)]
        )
    )
    diag_parent = dinv_parent - first_terms[0]
    cross_child = -(lead_product(link_block, diag_parent) + first_terms[1].T)
    child_partial = child_partial + lead_product(link_share, parent_share)
    child_share, child_part = row_total(child_partial, child_cols, row_index, share)
    second_terms = total_terms(jnp.stack([column_terms(child_part, child_blocks)]))
    diag_child = dinv_child - plain_product(cross_child, link_block) - second_terms[0]
    start = row_index * share
    return (
        parent_share,
        lax.dynamic_slice_in_dim(diag_parent, start, share, 0),
        lax.dynamic_slice_in_dim(cross_child, start, share, 0),
        child_share,
        lax.dynamic_slice_in_dim(diag_child, start, share, 0),
    )


def solution(mesh):
    return jax.shard_map(
        on_device,
        mesh=mesh,
        in_specs=(P("prow", "pcol"), P("prow", "pcol"), P("prow", "pcol"), P(), P(), P(), P(), P()),
        out_specs=(
            P("prow", "pcol"),
            P("prow", None),
            P("prow", None),
            P("prow", "pcol"),
            P("prow", None),
        ),
        check_vma=False,
    )
```

profile of v0, /device:TPU:0, one launch (start us, length us, event | category | flops | bytes accessed | tf_op | source)
XLA Modules:
  0.0 260.4 jit_solution(992268018349741853)
XLA Ops:
  7.2 0.0 copy-start
  7.2 0.0 all-reduce.5.cloned.1.call-start
  7.2 0.0 copy-start.6
  7.2 0.0 copy-start.7
  7.3 0.7 copy-done.6
  7.9 0.0 copy-done.7
  8.0 0.1 dynamic-slice_convert_fusion
  8.0 0.1 broadcast_bitcast_fusion.1
  8.1 33.2 %all_gather.6 = f32[512,256]{0,1:T(8,128)S(1)} all-gather(f32[512,32]{0,1:T(8,128)} %param.9), channel_id=1, replica_groups=mesh['prow'=4,'pcol'=8] {'pcol'}, dimensions={1}, use_global_device_ids=true | all-gather | bytes 589824 | tf_op jit(solution)/shard_map/all_gather | solution.py:59
  41.4 0.1 broadcast_multiply_fusion.1
  41.4 0.0 copy-done
  41.4 1.3 fusion.13
  42.7 0.0 all-reduce.5.cloned.1.call-update
  42.7 0.0 copy-start.5
  42.8 0.0 all-reduce.7.cloned.1.call-start
  42.8 0.6 dynamic_slice.45
  43.4 0.6 dynamic_slice.37
  45.3 0.1 broadcast_bitcast_fusion
  45.4 0.0 copy-done.5
  45.4 31.2 %all_gather.7 = f32[512,256]{0,1:T(8,128)S(1)} all-gather(f32[512,32]{0,1:T(8,128)S(1)} %copy-done.5), channel_id=1, replica_groups=mesh['prow'=4,'pcol'=8] {'pcol'}, dimensions={1}, use_global_device_ids=true | all-gather | bytes 589824 | tf_op jit(solution)/shard_map/all_gather | solution.py:60
  76.6 0.1 broadcast_multiply_fusion
  76.6 0.6 fusion.14
  77.2 0.0 all-reduce.5.cloned.1.call-done
  77.2 0.0 copy-start.1
  77.3 1.0 negate_multiply_fusion.1
  78.3 0.0 copy-done.1
  78.3 0.0 copy-start.4
  78.3 1.1 convolution_add_fusion
  79.5 0.0 copy-done.4
  79.5 0.0 all-reduce.7.cloned.1.call-update
  79.5 0.0 all-reduce.9.cloned.1.call-start
  79.5 0.4 convolution_bitcast_fusion.1
  80.0 0.4 convolution_bitcast_fusion
  80.4 0.8 pad_maximum_fusion
  81.2 32.0 %all-reduce.7.cloned.1.call-done = f32[256,256]{1,0:T(8,128)} async-done(((f32[256,256]{1,0:T(8,128)}), f32[256,256]{1,0:T(8,128)}) %all-reduce.7.cloned.1.call-update) | async-done | bytes 262160 | tf_op jit(solution)/shard_map/psum | solution.py:25
  113.2 1.0 negate_multiply_fusion
  114.2 1.1 fusion.4
  115.3 0.0 all-reduce.9.cloned.1.call-update
  115.3 0.6 constant_dynamic-slice_fusion
  116.0 132.6 %all-reduce.9.cloned.1.call-done = (f32[2,256,256]{2,1,0:T(8,128)}, f32[256,256]{1,0:T(8,128)}) async-done(((f32[2,256,256]{2,1,0:T(8,128)}, f32[256,256]{1,0:T(8,128)}), (f32[2,256,256]{2,1,0:T(8,128)}, f32[256,256]{1,0:T(8,128)})) %all-reduce.9.cloned.1.call-update) | async-done | bytes 786448 | tf_op jit(solution)/shard_map/psum | solution.py:31
  248.6 1.1 fusion.1
  249.6 0.1 copy-done.2
  249.7 0.6 fusion
  250.3 0.6 constant_dynamic-slice_fusion.1
  250.9 0.1 dynamic-slice_bitcast_fusion
  251.0 0.6 fusion.15
  251.6 0.7 copy.14
  252.3 1.5 dynamic-slice_subtract_fusion
  (6 shorter events, 0.0 us)
Async XLA Ops:
  7.2 34.3 %copy-start = (f32[512,256]{1,0:T(8,128)S(1)}, f32[512,256]{1,0:T(8,128)}, u32[]{:S(2)}) copy-start(f32[512,256]{1,0:T(8,128)} %param.8) | copy-start | bytes 1572868
  7.2 70.1 %all-reduce.5.cloned.1.call-start = ((), (), s32[]{:S(2)}) async-start(), calls=%async_computation | async-start | bytes 524288 | tf_op jit(solution)/shard_map/psum | solution.py:25
  7.2 0.7 copy-start.6
  7.2 0.7 copy-start.7
  42.7 2.6 %copy-start.5 = (f32[512,32]{0,1:T(8,128)S(1)}, f32[512,32]{0,1:T(8,128)}, u32[]{:S(2)}) copy-start(f32[512,32]{0,1:T(8,128)} %param.10) | copy-start | bytes 196612
  42.8 70.5 %all-reduce.7.cloned.1.call-start = ((), (), s32[]{:S(2)}) async-start(), calls=%async_computation.1 | async-start | bytes 524288 | tf_op jit(solution)/shard_map/psum | solution.py:25
  77.2 1.1 copy-start.1
  78.3 1.1 copy-start.4
  79.5 169.1 %all-reduce.9.cloned.1.call-start = ((), (), s32[]{:S(2)}) async-start(), calls=%async_computation.2 | async-start | bytes 1572864 | tf_op jit(solution)/shard_map/psum | solution.py:31
  115.3 133.3 %copy-start.3 = (f32[256,256]{1,0:T(8,128)S(1)}, f32[256,256]{1,0:T(8,128)}, u32[]{:S(2)}) copy-start(f32[256,256]{1,0:T(8,128)} %param.12) | copy-start | bytes 786436
  248.6 1.1 copy-start.2
Sparse Core Ops, SparseCore 0:
  42.9 33.3 all-reduce.4
  79.6 33.5 all-reduce.6
  118.5 130.0 all-reduce.8
where the time goes:
time: 261 us; the launch traced here: 260 us
  waiting for transfers between devices  165 us (63%)
  blocking collectives  64.4 us (25%)
  between operations  15.2 us (6%)
  matrix products  6.15 us (2%)
  other arithmetic  5.56 us (2%)
  local copies, waits for them, and re-layouts  4.23 us (2%)
    psum x1, waiting for transfers between devices, total_terms(): return lax.psum(stacked, ('prow', 'pcol'))  133 us
    all_gather x1, blocking collectives, on_device(): lax.all_gather(panel_parent, 'pcol', axis=1, tiled=True)  33.2 us
    psum x2, waiting for transfers between devices, row_total(): total = lax.psum(partial_value, 'prow')  32 us
    all_gather x1, blocking collectives, on_device(): lax.all_gather(panel_child, 'pcol', axis=1, tiled=True)  31.2 us
  transfers between devices with their start and end apart: 3, of which 2 were waited for; matrix products, arithmetic and copies ran while one was open for 2% of the time, Pallas kernels for 0%

commit v1 on v0

--- a/solution.py
+++ b/solution.py
@@ -4,6 +4,19 @@
 from jax.sharding import PartitionSpec as P
 
 highest = lax.Precision.HIGHEST
+
+
+def gather_around(x, axis, dim):
+    ways = lax.axis_size(axis)
+    up = [(d, (d + 1) % ways) for d in range(ways)]
+    down = [(d, (d - 1) % ways) for d in range(ways)]
+    earlier, later = ([x], [x])
+    for _ in range(ways // 2):
+        earlier.append(lax.ppermute(earlier[-1], axis, up))
+    for _ in range((ways - 1) // 2):
+        later.append(lax.ppermute(later[-1], axis, down))
+    line = jnp.concatenate([*earlier[::-1], *later[1:]], axis=dim)
+    return jnp.roll(line, (lax.axis_index(axis) - ways // 2) * x.shape[dim], axis=dim)
 
 
 def lead_product(left, right):
@@ -56,7 +69,7 @@
     first_row = row_index * row_blocks
     first_col = col_index * col_blocks
     parent_whole, child_whole = (
-        lax.all_gather(panel_parent, "pcol", axis=1, tiled=True),
+        gather_around(panel_parent, "pcol", 1),
         lax.all_gather(panel_child, "pcol", axis=1, tiled=True),
     )
     parent_rows = parent_whole * block_mask(pattern_parent, first_row, row_blocks, width)[:, None]

time: 261 us -> 287 us (1.100)
  waiting for transfers between devices: 165 us -> 207 us
  blocking collectives: 64.4 us -> 31.8 us
  starting transfers between devices: 0.12 us -> 15.8 us
    all_gather x1 -> x0, blocking collectives: 33.2 us -> none  [on_device(): lax.all_gather(panel_parent, 'pcol', axis=1, tiled=True)]
    psum x2, waiting for transfers between devices: 32 us -> 64.4 us  [row_total(): total = lax.psum(partial_value, 'prow')]
    ppermute x0 -> x7, starting transfers between devices: none -> 15.7 us  [the longest x3 12.6 us: gather_around(): later.append(lax.ppermute(later[-1], axis, down))]
    ppermute x0 -> x7, waiting for transfers between devices: none -> 9.99 us  [the longest x4 9 us: gather_around(): earlier.append(lax.ppermute(earlier[-1], axis, up))]
  transfers between devices with their start and end apart: 3 -> 10, of which waited for: 2 -> 6; matrix products, arithmetic and copies ran while one was open for 2% -> 2% of each run, Pallas kernels for 0% -> 0%
where the time goes in v1:
time: 287 us
  waiting for transfers between devices  207 us (72%)
  blocking collectives  31.8 us (11%)
  starting transfers between devices  15.8 us (6%)
  between operations  15.3 us (5%)
  matrix products  6.16 us (2%)
  other arithmetic  5.57 us (2%)
  local copies, waits for them, and re-layouts  5.05 us (2%)
    psum x1, waiting for transfers between devices, total_terms(): return lax.psum(stacked, ('prow', 'pcol'))  133 us
    psum x2, waiting for transfers between devices, row_total(): total = lax.psum(partial_value, 'prow')  64.4 us
    all_gather x1, blocking collectives, on_device(): lax.all_gather(panel_child, 'pcol', axis=1, tiled=True)  31.8 us
    ppermute x3, starting transfers between devices, gather_around(): later.append(lax.ppermute(later[-1], axis, down))  12.6 us
    ppermute x4, waiting for transfers between devices, gather_around(): earlier.append(lax.ppermute(earlier[-1], axis, up))  9 us
  transfers between devices with their start and end apart: 10, of which 6 were waited for; matrix products, arithmetic and copies ran while one was open for 2% of the time, Pallas kernels for 0%

profile of v1, /device:TPU:0, one launch (start us, length us, event | category | flops | bytes accessed | tf_op | source)
XLA Modules:
  0.0 286.7 jit_solution(12763648844551591764)
XLA Ops:
  7.2 0.0 copy-start
  7.2 0.0 all-reduce.5.cloned.1.call-start
  7.2 3.0 %collective-permute-start = (f32[512,32]{0,1:T(8,128)}, f32[512,32]{0,1:T(8,128)S(1)}, u32[]{:S(2)}, u32[]{:S(2)}) collective-permute-start(f32[512,32]{0,1:T(8,128)} %param.9), channel_id=1, source_target_pairs={{0,1},{1,2},{2,3},{3,4},{4,5},{5,6},{6,7},{7,0},{8,9},{9,10},{10,1... | collective-permute-start | bytes 196616 | tf_op jit(solution)/shard_map/ppermute | solution.py:15
  10.2 3.1 %collective-permute-start.4 = (f32[512,32]{0,1:T(8,128)}, f32[512,32]{0,1:T(8,128)S(1)}, u32[]{:S(2)}, u32[]{:S(2)}) collective-permute-start(f32[512,32]{0,1:T(8,128)} %param.9), channel_id=1, source_target_pairs={{0,7},{1,0},{2,1},{3,2},{4,3},{5,4},{6,5},{7,6},{8,15},{9,8},{10,9... | collective-permute-start | bytes 196616 | tf_op jit(solution)/shard_map/ppermute | solution.py:17
  13.4 31.8 %all_gather.3 = f32[512,256]{0,1:T(8,128)S(1)} all-gather(f32[512,32]{0,1:T(8,128)} %param.10), channel_id=1, replica_groups=mesh['prow'=4,'pcol'=8] {'pcol'}, dimensions={1}, use_global_device_ids=true | all-gather | bytes 589824 | tf_op jit(solution)/shard_map/all_gather | solution.py:73
  45.1 0.7 copy-done.6
  45.8 0.0 copy-done.7
  45.8 0.1 dynamic-slice_convert_fusion
  45.9 0.0 collective-permute-done
  45.9 0.0 collective-permute-start.1
  45.9 0.1 broadcast_bitcast_fusion
  45.9 6.9 %collective-permute-done.1 = f32[512,32]{0,1:T(8,128)S(1)} collective-permute-done((f32[512,32]{0,1:T(8,128)S(1)}, f32[512,32]{0,1:T(8,128)S(1)}, u32[]{:S(2)}, u32[]{:S(2)}) %collective-permute-start.1) | collective-permute-done | bytes 65568 | tf_op jit(solution)/shard_map/ppermute | solution.py:15
  52.8 0.1 broadcast_multiply_fusion
  52.9 4.8 %collective-permute-start.5 = (f32[512,32]{0,1:T(8,128)S(1)}, f32[512,32]{0,1:T(8,128)S(1)}, u32[]{:S(2)}, u32[]{:S(2)}) collective-permute-start(f32[512,32]{0,1:T(8,128)S(1)} %collective-permute-done.4), channel_id=1, source_target_pairs={{0,7},{1,0},{2,1},{3,2},{4,3},{5,4},{6,5},{7,6},{8,15},{9,8},{10,9... | collective-permute-start | bytes 196616 | tf_op jit(solution)/shard_map/ppermute | solution.py:17
  57.7 2.1 collective-permute-done.2
  59.8 0.1 broadcast_bitcast_fusion.1
  59.9 0.6 dynamic_slice.42
  60.4 0.6 dynamic_slice.50
  62.4 4.8 %collective-permute-start.6 = (f32[512,32]{0,1:T(8,128)S(1)}, f32[512,32]{0,1:T(8,128)S(1)}, u32[]{:S(2)}, u32[]{:S(2)}) collective-permute-start(f32[512,32]{0,1:T(8,128)S(1)} %collective-permute-done.5), channel_id=1, source_target_pairs={{0,7},{1,0},{2,1},{3,2},{4,3},{5,4},{6,5},{7,6},{8,15},{9,8},{10,9... | collective-permute-start | bytes 196616 | tf_op jit(solution)/shard_map/ppermute | solution.py:17
  67.2 0.0 copy-start.5
  67.2 0.8 copy-done.5
  68.1 1.0 collective-permute-done.6
  69.2 1.3 fusion.13
  70.5 0.0 all-reduce.5.cloned.1.call-update
  70.5 0.0 all-reduce.7.cloned.1.call-start
  70.6 0.6 fusion.14
  71.2 33.8 %all-reduce.5.cloned.1.call-done = f32[256,256]{1,0:T(8,128)} async-done(((f32[256,256]{1,0:T(8,128)}), f32[256,256]{1,0:T(8,128)}) %all-reduce.5.cloned.1.call-update) | async-done | bytes 262160 | tf_op jit(solution)/shard_map/psum | solution.py:38
  105.0 1.0 negate_multiply_fusion.1
  106.0 0.0 copy-start.4
  106.0 1.1 convolution_add_fusion
  107.1 0.0 all-reduce.7.cloned.1.call-update
  107.2 0.0 all-reduce.9.cloned.1.call-start
  107.2 0.4 convolution_bitcast_fusion
  107.7 0.4 convolution_bitcast_fusion.1
  108.1 0.8 pad_maximum_fusion
  108.9 30.7 %all-reduce.7.cloned.1.call-done = f32[256,256]{1,0:T(8,128)} async-done(((f32[256,256]{1,0:T(8,128)}), f32[256,256]{1,0:T(8,128)}) %all-reduce.7.cloned.1.call-update) | async-done | bytes 262160 | tf_op jit(solution)/shard_map/psum | solution.py:38
  139.6 1.0 negate_multiply_fusion
  140.6 1.1 fusion.4
  141.7 0.0 all-reduce.9.cloned.1.call-update
  141.7 0.6 constant_dynamic-slice_fusion
  142.4 132.6 %all-reduce.9.cloned.1.call-done = (f32[2,256,256]{2,1,0:T(8,128)}, f32[256,256]{1,0:T(8,128)}) async-done(((f32[2,256,256]{2,1,0:T(8,128)}, f32[256,256]{1,0:T(8,128)}), (f32[2,256,256]{2,1,0:T(8,128)}, f32[256,256]{1,0:T(8,128)})) %all-reduce.9.cloned.1.call-update) | async-done | bytes 786448 | tf_op jit(solution)/shard_map/psum | solution.py:44
  274.9 1.1 fusion.1
  276.0 0.6 constant_dynamic-slice_fusion.1
  276.6 0.6 fusion
  277.2 0.1 dynamic-slice_bitcast_fusion
  277.4 0.6 fusion.15
  278.0 0.7 copy.14
  278.7 1.5 dynamic-slice_subtract_fusion
  (35 shorter events, 0.2 us)
Async XLA Ops:
  7.2 62.1 %copy-start = (f32[512,256]{1,0:T(8,128)S(1)}, f32[512,256]{1,0:T(8,128)}, u32[]{:S(2)}) copy-start(f32[512,256]{1,0:T(8,128)} %param.8) | copy-start | bytes 1572868
  7.2 97.8 %all-reduce.5.cloned.1.call-start = ((), (), s32[]{:S(2)}) async-start(), calls=%async_computation | async-start | bytes 524288 | tf_op jit(solution)/shard_map/psum | solution.py:38
  7.2 38.6 %collective-permute-start = (f32[512,32]{0,1:T(8,128)}, f32[512,32]{0,1:T(8,128)S(1)}, u32[]{:S(2)}, u32[]{:S(2)}) collective-permute-start(f32[512,32]{0,1:T(8,128)} %param.9), channel_id=1, source_target_pairs={{0,1},{1,2},{2,3},{3,4},{4,5},{5,6},{6,7},{7,0},{8,9},{9,10},{10,1... | collective-permute-start | bytes 196616 | tf_op jit(solution)/shard_map/ppermute | solution.py:15
  10.2 42.6 %collective-permute-start.4 = (f32[512,32]{0,1:T(8,128)}, f32[512,32]{0,1:T(8,128)S(1)}, u32[]{:S(2)}, u32[]{:S(2)}) collective-permute-start(f32[512,32]{0,1:T(8,128)} %param.9), channel_id=1, source_target_pairs={{0,7},{1,0},{2,1},{3,2},{4,3},{5,4},{6,5},{7,6},{8,15},{9,8},{10,9... | collective-permute-start | bytes 196616 | tf_op jit(solution)/shard_map/ppermute | solution.py:17
  45.1 0.7 copy-start.6
  45.1 0.7 copy-start.7
  45.9 7.0 %collective-permute-start.1 = (f32[512,32]{0,1:T(8,128)S(1)}, f32[512,32]{0,1:T(8,128)S(1)}, u32[]{:S(2)}, u32[]{:S(2)}) collective-permute-start(f32[512,32]{0,1:T(8,128)S(1)} %collective-permute-done), channel_id=1, source_target_pairs={{0,1},{1,2},{2,3},{3,4},{4,5},{5,6},{6,7},{7,0},{8,9},{9,10},{10,1... | collective-permute-start | bytes 196616 | tf_op jit(solution)/shard_map/ppermute | solution.py:15
  52.8 7.0 %collective-permute-start.2 = (f32[512,32]{0,1:T(8,128)S(1)}, f32[512,32]{0,1:T(8,128)S(1)}, u32[]{:S(2)}, u32[]{:S(2)}) collective-permute-start(f32[512,32]{0,1:T(8,128)S(1)} %collective-permute-done.1), channel_id=1, source_target_pairs={{0,1},{1,2},{2,3},{3,4},{4,5},{5,6},{6,7},{7,0},{8,9},{9,10},{10,1... | collective-permute-start | bytes 196616 | tf_op jit(solution)/shard_map/ppermute | solution.py:15
  52.9 9.5 %collective-permute-start.5 = (f32[512,32]{0,1:T(8,128)S(1)}, f32[512,32]{0,1:T(8,128)S(1)}, u32[]{:S(2)}, u32[]{:S(2)}) collective-permute-start(f32[512,32]{0,1:T(8,128)S(1)} %collective-permute-done.4), channel_id=1, source_target_pairs={{0,7},{1,0},{2,1},{3,2},{4,3},{5,4},{6,5},{7,6},{8,15},{9,8},{10,9... | collective-permute-start | bytes 196616 | tf_op jit(solution)/shard_map/ppermute | solution.py:17
  59.8 7.4 %collective-permute-start.3 = (f32[512,32]{0,1:T(8,128)S(1)}, f32[512,32]{0,1:T(8,128)S(1)}, u32[]{:S(2)}, u32[]{:S(2)}) collective-permute-start(f32[512,32]{0,1:T(8,128)S(1)} %collective-permute-done.2), channel_id=1, source_target_pairs={{0,1},{1,2},{2,3},{3,4},{4,5},{5,6},{6,7},{7,0},{8,9},{9,10},{10,1... | collective-permute-start | bytes 196616 | tf_op jit(solution)/shard_map/ppermute | solution.py:15
  62.4 6.7 %collective-permute-start.6 = (f32[512,32]{0,1:T(8,128)S(1)}, f32[512,32]{0,1:T(8,128)S(1)}, u32[]{:S(2)}, u32[]{:S(2)}) collective-permute-start(f32[512,32]{0,1:T(8,128)S(1)} %collective-permute-done.5), channel_id=1, source_target_pairs={{0,7},{1,0},{2,1},{3,2},{4,3},{5,4},{6,5},{7,6},{8,15},{9,8},{10,9... | collective-permute-start | bytes 196616 | tf_op jit(solution)/shard_map/ppermute | solution.py:17
  67.2 0.8 copy-start.5
  70.5 69.1 %all-reduce.7.cloned.1.call-start = ((), (), s32[]{:S(2)}) async-start(), calls=%async_computation.1 | async-start | bytes 524288 | tf_op jit(solution)/shard_map/psum | solution.py:38
  105.0 1.0 copy-start.1
  106.0 1.1 copy-start.4
  107.2 167.8 %all-reduce.9.cloned.1.call-start = ((), (), s32[]{:S(2)}) async-start(), calls=%async_computation.2 | async-start | bytes 1572864 | tf_op jit(solution)/shard_map/psum | solution.py:44
  141.7 133.2 %copy-start.3 = (f32[256,256]{1,0:T(8,128)S(1)}, f32[256,256]{1,0:T(8,128)}, u32[]{:S(2)}) copy-start(f32[256,256]{1,0:T(8,128)} %param.12) | copy-start | bytes 786436
  274.9 1.7 copy-start.2
Sparse Core Ops, SparseCore 0:
  70.7 34.2 all-reduce.4
  107.3 32.2 all-reduce.6
  144.9 130.0 all-reduce.8
